TPU v7x, 256 devices: a whole 4x4x8 slice. The times are simulated.
256 devices in a mesh: fsdp: 32 (over z, y), tensor: 8 (over x, core).
Axes of the slice: x: 4, y: 4, z: 8, core: 2. Of those that a mesh axis runs over, the one named last changes fastest.
Arguments:
- context: bfloat16 [8192, 4096], P('fsdp', 'tensor'), may hold values from -6 to 6
- cotangent: bfloat16 [8192, 8192], P('fsdp', 'tensor'), may hold values from -0.0625 to 0.0625
- block_table: int32 [8, 64], P('tensor'), may hold values from 0 to 63, each once within a row
- left_stat: float32 [8, 64, 256, 256], P('tensor', 'fsdp'), may hold values from -1 to 5, as said below
- right_stat: float32 [8, 64, 256, 256], P('tensor', 'fsdp'), may hold values from -1 to 5, as said below
- root_left: float32 [8, 64, 256, 256], P('tensor', 'fsdp'), may hold values from -1 to 5, as said below
- root_right: float32 [8, 64, 256, 256], P('tensor', 'fsdp'), may hold values from -1 to 5, as said below
- second_moment: float32 [8, 64, 256, 256], P('tensor', 'fsdp'), may hold values from 0.3 to 3
Outputs:
- left_new: float32 [8, 64, 256, 256], P('tensor', 'fsdp')
- right_new: float32 [8, 64, 256, 256], P('tensor', 'fsdp')
- second_new: float32 [8, 64, 256, 256], P('tensor', 'fsdp')
- search_direction: bfloat16 [8, 512, 8192], P('tensor', 'fsdp')
Inputs may be any that keep to these rules, and one draw needn't show every extreme that they name: Each row of block_table names every block 0 to 63 once. `left_stat`: symmetric, with positive diagonal. `right_stat`: symmetric, with positive diagonal. `root_left`: symmetric, with positive diagonal. `root_right`: symmetric, with positive diagonal.
All inputs are finite; a program needn't handle non-finite values.
Results may differ from a plain program's by a relative error of at most 0.017.
Values may be sent and summed in bfloat16 or wider, within the bound.
A program may use at most 128 MiB of HBM per device.

v0:
```python
import jax
import jax.numpy as jnp
from jax import lax
from jax.sharding import Mesh
from jax.sharding import PartitionSpec as P

FSDP = ("fsdp_0", "fsdp_1")
decay_rate = 0.95


def own_rows(terms, axes):
    total = terms.astype(jnp.bfloat16)
    for axis in axes:
        total = lax.psum_scatter(total, axis, scatter_dimension=0, tiled=True)
    return total.astype(jnp.float32)


def per_device(
    context, cotangent, block_table, left_stat, right_stat, root_left, root_right, second_moment
):
    full_cot = lax.all_gather(cotangent, "tensor", axis=1, tiled=True)
    tokens_here, band_rows = context.shape
    model_width = full_cot.shape[1]
    block_size = left_stat.shape[-1]
    slot_count = left_stat.shape[1]
    groups = lax.axis_size(FSDP)
    position = lax.axis_index(FSDP)
    owner_table = block_table[0]
    col_bands = model_width // block_size
    strip_rows = band_rows // groups
    per_band = block_size // strip_rows
    my_blocks = lax.dynamic_slice_in_dim(owner_table, position * slot_count, slot_count)
    ctx_bands = context.reshape(tokens_here, band_rows // block_size, block_size)
    cot_bands = full_cot.reshape(tokens_here, col_bands, block_size)
    left_part = jnp.take(ctx_bands, owner_table // col_bands, axis=1)
    right_part = jnp.take(cot_bands, owner_table % col_bands, axis=1)
    blocks = jnp.einsum("tnb,tnc->nbc", left_part, right_part, preferred_element_type=jnp.float32)
    gradient = own_rows(
        blocks.reshape(slot_count * block_size * lax.axis_size(FSDP), block_size), FSDP
    )
    gradient = gradient.reshape(slot_count, block_size, block_size)
    highest = lax.Precision.HIGHEST
    gram_left = jnp.einsum("sij,skj->sik", gradient, gradient, precision=highest)
    gram_right = jnp.einsum("sji,sjk->sik", gradient, gradient, precision=highest)
    left_new = decay_rate * left_stat[0] + (1.0 - decay_rate) * gram_left / block_size
    right_new = decay_rate * right_stat[0] + (1.0 - decay_rate) * gram_right / block_size
    second_new = decay_rate * second_moment[0] + (1.0 - decay_rate) * gradient * gradient
    adam_step = gradient / (jnp.sqrt(second_new) + 1e-08)
    shaped = jnp.einsum("sij,sjk->sik", root_left[0], gradient, precision=highest)
    shaped = jnp.einsum("sij,sjk->sik", shaped, root_right[0], precision=highest)
    graft_ratio = jnp.sqrt(jnp.sum(adam_step * adam_step, axis=(1, 2))) / jnp.sqrt(
        jnp.sum(shaped * shaped, axis=(1, 2)) + 1e-06
    )
    direction = (shaped * graft_ratio[:, None, None]).astype(jnp.bfloat16)
    by_strip = direction.reshape(slot_count, per_band, strip_rows, block_size)
    targets = jnp.arange(groups, dtype=jnp.int32)
    chosen = jnp.take(by_strip, targets % per_band, axis=1)
    keep_mask = ((my_blocks // col_bands)[:, None] == (targets // per_band)[None, :]).astype(
        jnp.bfloat16
    )
    outgoing_rows = jnp.swapaxes(chosen * keep_mask[:, :, None, None], 0, 1)
    returned = lax.all_to_all(outgoing_rows, FSDP, split_axis=0, concat_axis=0, tiled=True)
    wanted = position // per_band * col_bands + jnp.arange(col_bands, dtype=jnp.int32)
    slot_ids = jnp.arange(owner_table.shape[0], dtype=jnp.int32)
    located = jnp.sum(
        jnp.where(owner_table[None, :] == wanted[:, None], slot_ids[None, :], 0), axis=1
    )
    flat_pieces = returned.reshape(groups * slot_count, strip_rows, block_size)
    pieces = jnp.take(flat_pieces, located, axis=0)
    result = jnp.swapaxes(pieces, 0, 1).reshape(strip_rows, model_width)
    return (left_new[None], right_new[None], second_new[None], result[None])


def solution(mesh):
    finer = Mesh(mesh.devices.reshape(8, 4, mesh.shape["tensor"]), ("fsdp_0", "fsdp_1", "tensor"))
    in_specs = (
        P(FSDP, "tensor"),
        P(FSDP, "tensor"),
        P("tensor", None),
        P("tensor", FSDP, None, None),
        P("tensor", FSDP, None, None),
        P("tensor", FSDP, None, None),
        P("tensor", FSDP, None, None),
        P("tensor", FSDP, None, None),
    )
    out_specs = (
        P("tensor", FSDP, None, None),
        P("tensor", FSDP, None, None),
        P("tensor", FSDP, None, None),
        P("tensor", FSDP, None),
    )
    return jax.shard_map(
        per_device, mesh=finer, in_specs=in_specs, out_specs=out_specs, check_vma=False
    )
```

profile of v0, /device:TPU:2, one launch (start us, length us, event | category | flops | bytes accessed | tf_op | source)
XLA Modules:
  0.0 236.2 jit_solution(10105942067028597240)
XLA Ops:
  7.2 0.0 copy-start
  7.2 0.0 all-gather.2.cloned.1.call-start
  7.2 2.1 copy.38
  9.3 0.0 all-gather.2.cloned.1.call-update
  9.3 0.0 reduce-scatter.3.cloned.1.call-start
  9.4 1.1 copy.36
  10.5 0.1 copy.37
  10.6 0.7 fusion.28
  11.3 0.0 copy-start.6
  11.3 5.4 %gather_fusion = bf16[64,256,256]{2,1,0:T(8,128)(2,1)} fusion(bf16[256,2,256]{2,0,1:T(8,128)(2,1)S(1)} %copy.37, s32[1024]{0:T(1024)S(1)} %get-tuple-element.13), kind=kCustom, calls=%fused_computation | custom fusion | bytes 16777472 | tf_op jit(solution)/shard_map/jit(_take)/gather | solution.py:35
  16.7 0.0 copy-done.6
  16.7 30.3 %all-gather.2.cloned.1.call-done = bf16[256,8192]{0,1:T(8,128)(2,1)} async-done(((bf16[256,1024]{0,1:T(8,128)(2,1)}), bf16[256,8192]{0,1:T(8,128)(2,1)}) %all-gather.2.cloned.1.call-update) | async-done | bytes 4194320 | tf_op jit(solution)/shard_map/all_gather | solution.py:21
  47.0 6.4 %copy.39 = bf16[256,32,256]{2,0,1:T(8,128)(2,1)} copy(bf16[256,32,256]{0,2,1:T(8,128)(2,1)} %bitcast.93) | data formatting | bytes 8388608 | tf_op jit(solution)/shard_map/reshape | solution.py:34
  53.4 7.7 %gather_fusion.1 = bf16[64,256,256]{2,1,0:T(8,128)(2,1)} fusion(bf16[256,32,256]{2,0,1:T(8,128)(2,1)} %copy.39, s32[1024]{0:T(1024)S(1)} %get-tuple-element.12), kind=kCustom, calls=%fused_computation.1 | custom fusion | bytes 16777472 | tf_op jit(solution)/shard_map/jit(_take)/gather | solution.py:36
  61.1 11.4 %fusion.7 = bf16[64,256,256]{2,1,0:T(8,128)(2,1)} fusion(bf16[64,256,256]{2,1,0:T(8,128)(2,1)} %gather_fusion.1, pred[64]{0:T(512)(128)(4,1)S(1)} %get-tuple-element.7, bf16[64,256,256]{2,1,0:T(8,128)(2,1)} %gather_fusion, pred[64]{0:T(512)(128)(4,1)S(1)} %get-tuple-element.6), kind=kOutput, calls=%fused_computation.11 | convolution fusion | flops 2160066560 | bytes 25165952 | tf_op jit(solution)/shard_map/tnb,tnc->nbc/dot_general | solution.py:37
  72.5 0.0 copy-start.2
  72.5 0.0 copy-start.4
  72.5 0.0 reduce-scatter.3.cloned.1.call-update
  72.5 0.0 reduce-scatter.5.cloned.1.call-start
  72.6 96.0 %reduce-scatter.3.cloned.1.call-done = bf16[2048,256]{1,0:T(8,128)(2,1)} async-done(((bf16[16384,256]{1,0:T(8,128)(2,1)}), bf16[2048,256]{1,0:T(8,128)(2,1)}) %reduce-scatter.3.cloned.1.call-update) | async-done | bytes 1048592 | tf_op jit(solution)/shard_map/reduce_scatter | solution.py:14
  168.6 0.0 reduce-scatter.5.cloned.1.call-update
  168.6 0.1 and_select_fusion.1
  168.7 0.1 compare_convert_fusion
  168.8 0.1 copy.44
  168.9 27.3 %reduce-scatter.5.cloned.1.call-done = bf16[512,256]{1,0:T(8,128)(2,1)} async-done(((bf16[2048,256]{1,0:T(8,128)(2,1)}), bf16[512,256]{1,0:T(8,128)(2,1)}) %reduce-scatter.5.cloned.1.call-update) | async-done | bytes 262160 | tf_op jit(solution)/shard_map/reduce_scatter | solution.py:14
  196.2 0.0 copy-done.2
  196.2 1.9 broadcast_multiply_fusion
  198.1 1.3 fusion.27
  199.5 0.0 copy-done.5
  199.5 1.3 fusion.25
  200.8 0.0 copy-done
  200.8 0.8 multiply_reduce_fusion
  201.6 0.1 reduce_sum.39
  201.7 0.1 multiply_convert_fusion
  201.8 0.6 gather_fusion.2
  202.4 1.0 select_multiply_fusion
  203.4 8.2 %all-to-all-start = ((bf16[32,2,16,256]{3,2,1,0:T(8,128)(2,1)}), bf16[32,2,16,256]{3,2,1,0:T(8,128)(2,1)S(1)}, u32[]{:S(2)}, u32[]{:S(2)}) async-start(bf16[32,2,16,256]{3,2,1,0:T(8,128)(2,1)} %select_multiply_fusion), calls=%async_computation.2 | async-start | bytes 1048576 | tf_op jit(solution)/shard_map/all_to_all | solution.py:62
  211.7 0.2 select_reduce_fusion
  211.9 0.0 copy-done.3
  211.9 0.0 copy-done.1
  211.9 1.1 fusion.14
  213.0 0.0 copy-done.4
  213.0 1.1 fusion.16
  214.0 14.0 %all-to-all-done = bf16[32,2,16,256]{3,2,1,0:T(8,128)(2,1)S(1)} async-done(((bf16[32,2,16,256]{3,2,1,0:T(8,128)(2,1)}), bf16[32,2,16,256]{3,2,1,0:T(8,128)(2,1)S(1)}, u32[]{:S(2)}, u32[]{:S(2)}) %all-to-all-start) | async-done | bytes 524320 | tf_op jit(solution)/shard_map/all_to_all | solution.py:62
  228.1 0.6 gather_fusion.3
  228.7 0.1 select_bitcast_fusion
  228.8 0.1 copy.45
  228.9 0.8 broadcast_in_dim_reshape.3
  (15 shorter events, 0.1 us)
Async XLA Ops:
  7.2 193.7 %copy-start = (f32[1,2,256,256]{3,2,1,0:T(8,128)S(1)}, f32[1,2,256,256]{3,2,1,0:T(8,128)}, u32[]{:S(2)}) copy-start(f32[1,2,256,256]{3,2,1,0:T(8,128)} %param.14) | copy-start | bytes 1572868
  7.2 39.8 %all-gather.2.cloned.1.call-start = ((), (), s32[]{:S(2)}) async-start(), calls=%async_computation.3 | async-start | bytes 4718592 | tf_op jit(solution)/shard_map/all_gather | solution.py:21
  9.3 159.3 %reduce-scatter.3.cloned.1.call-start = ((), (), s32[]{:S(2)}) async-start(), calls=%async_computation.4 | async-start | bytes 9437184 | tf_op jit(solution)/shard_map/reduce_scatter | solution.py:14
  11.3 5.4 %copy-start.6 = (s32[1,64]{1,0:T(1,128)S(1)}, s32[1,64]{1,0:T(1,128)}, u32[]{:S(2)}) copy-start(s32[1,64]{1,0:T(1,128)} %param.10) | copy-start | bytes 772
  72.5 123.7 %copy-start.2 = (f32[1,2,256,256]{3,2,1,0:T(8,128)S(1)}, f32[1,2,256,256]{3,2,1,0:T(8,128)}, u32[]{:S(2)}) copy-start(f32[1,2,256,256]{3,2,1,0:T(8,128)} %param.15) | copy-start | bytes 1572868
  72.5 127.0 %copy-start.5 = (f32[1,2,256,256]{3,2,1,0:T(8,128)S(1)}, f32[1,2,256,256]{3,2,1,0:T(8,128)}, u32[]{:S(2)}) copy-start(f32[1,2,256,256]{3,2,1,0:T(8,128)} %param.13) | copy-start | bytes 1572868
  72.5 139.4 %copy-start.3 = (f32[1,2,256,256]{3,2,1,0:T(8,128)S(1)}, f32[1,2,256,256]{3,2,1,0:T(8,128)}, u32[]{:S(2)}) copy-start(f32[1,2,256,256]{3,2,1,0:T(8,128)} %param.12) | copy-start | bytes 1572868
  72.5 140.5 %copy-start.4 = (f32[1,2,256,256]{3,2,1,0:T(8,128)S(1)}, f32[1,2,256,256]{3,2,1,0:T(8,128)}, u32[]{:S(2)}) copy-start(f32[1,2,256,256]{3,2,1,0:T(8,128)} %param.11) | copy-start | bytes 1572868
  72.5 123.7 %reduce-scatter.5.cloned.1.call-start = ((), (), s32[]{:S(2)}) async-start(), calls=%async_computation.5 | async-start | bytes 1310720 | tf_op jit(solution)/shard_map/reduce_scatter | solution.py:14
  196.2 15.7 %copy-start.1 = (bf16[512,256]{1,0:T(8,128)(2,1)S(1)}, bf16[512,256]{1,0:T(8,128)(2,1)}, u32[]{:S(2)}) copy-start(bf16[512,256]{1,0:T(8,128)(2,1)} %reduce-scatter.5.cloned.1.call-done) | copy-start | bytes 786436
  203.4 24.7 %all-to-all-start = ((bf16[32,2,16,256]{3,2,1,0:T(8,128)(2,1)}), bf16[32,2,16,256]{3,2,1,0:T(8,128)(2,1)S(1)}, u32[]{:S(2)}, u32[]{:S(2)}) async-start(bf16[32,2,16,256]{3,2,1,0:T(8,128)(2,1)} %select_multiply_fusion), calls=%async_computation.2 | async-start | bytes 1048576 | tf_op jit(solution)/shard_map/all_to_all | solution.py:62
Sparse Core Ops, SparseCore 0:
  10.4 36.5 all-gather.1
  72.7 95.8 reduce-scatter.2
  171.1 25.0 reduce-scatter.4
where the time goes:
time: 237 us; the launch traced here: 236 us
  waiting for transfers between devices  168 us (71%)
  local copies, waits for them, and re-layouts  25 us (11%)
  matrix products  15.6 us (7%)
  between operations  13.9 us (6%)
  starting transfers between devices  8.37 us (4%)
  other arithmetic  5.64 us (2%)
    reduce_scatter x2, waiting for transfers between devices, own_rows(): total = lax.psum_scatter(total, axis, scatter_dimension=0, tiled=True)  123 us
    all_gather x1, waiting for transfers between devices, per_device(): full_cot = lax.all_gather(cotangent, 'tensor', axis=1, tiled=True)  30.3 us
    all_to_all x1, waiting for transfers between devices, per_device(): lax.all_to_all(outgoing_rows, FSDP, split_axis=0, concat_axis=0, tiled=True)  14 us
    dot_general x1, matrix products, per_device(): jnp.einsum('tnb,tnc->nbc', left_part, right_part, preferred_element_type=...  11.4 us
    all_to_all x1, starting transfers between devices, per_device(): lax.all_to_all(outgoing_rows, FSDP, split_axis=0, concat_axis=0, tiled=True)  8.25 us
    gather x1, local copies, waits for them, and re-layouts, per_device(): right_part = jnp.take(cot_bands, owner_table % col_bands, axis=1)  7.71 us
    reshape x1, local copies, waits for them, and re-layouts, per_device(): cot_bands = full_cot.reshape(tokens_here, col_bands, block_size)  6.43 us
    gather x1, local copies, waits for them, and re-layouts, per_device(): left_part = jnp.take(ctx_bands, owner_table // col_bands, axis=1)  5.37 us
  transfers between devices with their start and end apart: 4, of which 4 were waited for; matrix products, arithmetic and copies ran while one was open for 4% of the time, Pallas kernels for 0%

commit v1 on v0

--- a/solution.py
+++ b/solution.py
@@ -18,7 +18,25 @@
 def per_device(
     context, cotangent, block_table, left_stat, right_stat, root_left, root_right, second_moment
 ):
-    full_cot = lax.all_gather(cotangent, "tensor", axis=1, tiled=True)
+    length, mine, span = (lax.axis_size("tensor"), lax.axis_index("tensor"), cotangent.shape[1])
+    right = [(i, (i + 1) % length) for i in range(length)]
+    backward = [(i, (i - 1) % length) for i in range(length)]
+    full_cot = jnp.zeros(
+        (*cotangent.shape[:1], length * span, *cotangent.shape[1 + 1 :]), cotangent.dtype
+    )
+    full_cot = lax.dynamic_update_slice_in_dim(full_cot, cotangent, mine * span, axis=1)
+    from_left = from_right = cotangent
+    halfway = length // 2
+    for step in range(1, halfway + 1):
+        from_left = lax.ppermute(from_left, "tensor", right)
+        full_cot = lax.dynamic_update_slice_in_dim(
+            full_cot, from_left, (mine - step) % length * span, axis=1
+        )
+        if step < length - halfway:
+            from_right = lax.ppermute(from_right, "tensor", backward)
+            full_cot = lax.dynamic_update_slice_in_dim(
+                full_cot, from_right, (mine + step) % length * span, axis=1
+            )
     tokens_here, band_rows = context.shape
     model_width = full_cot.shape[1]
     block_size = left_stat.shape[-1]

time: 237 us -> 242 us (1.021)
  waiting for transfers between devices: 168 us -> 158 us
  local copies, waits for them, and re-layouts: 25 us -> 34.2 us
  starting transfers between devices: 8.37 us -> 13.9 us
    all_gather x1 -> x0, waiting for transfers between devices: 30.3 us -> none  [per_device(): full_cot = lax.all_gather(cotangent, 'tensor', axis=1, tiled=True)]
    ppermute x0 -> x7, waiting for transfers between devices: none -> 17.8 us  [the longest x4 16.4 us: per_device(): from_left = lax.ppermute(from_left, 'tensor', right)]
    dynamic_update_slice x0 -> x8, local copies, waits for them, and re-layouts: none -> 7.75 us  [the longest x4 4.43 us: per_device(): lax.dynamic_update_slice_in_dim(full_cot, from_left, (mine - step) % leng...]
    ppermute x0 -> x7, starting transfers between devices: none -> 5.45 us  [the longest x3 5.43 us: per_device(): from_right = lax.ppermute(from_right, 'tensor', backward)]
    reduce_scatter x2, waiting for transfers between devices: 123 us -> 126 us  [own_rows(): total = lax.psum_scatter(total, axis, scatter_dimension=0, tiled=True)]
  transfers between devices with their start and end apart: 4 -> 10, of which waited for: 4 -> 7; matrix products, arithmetic and copies ran while one was open for 4% -> 8% of each run, Pallas kernels for 0% -> 0%
where the time goes in v1:
time: 242 us
  waiting for transfers between devices  158 us (65%)
  local copies, waits for them, and re-layouts  34.2 us (14%)
  matrix products  15.6 us (6%)
  between operations  14.4 us (6%)
  starting transfers between devices  13.9 us (6%)
  other arithmetic  5.63 us (2%)
    reduce_scatter x2, waiting for transfers between devices, own_rows(): total = lax.psum_scatter(total, axis, scatter_dimension=0, tiled=True)  126 us
    ppermute x4, waiting for transfers between devices, per_device(): from_left = lax.ppermute(from_left, 'tensor', right)  16.4 us
    all_to_all x1, waiting for transfers between devices, per_device(): lax.all_to_all(outgoing_rows, FSDP, split_axis=0, concat_axis=0, tiled=True)  14 us
    dot_general x1, matrix products, per_device(): jnp.einsum('tnb,tnc->nbc', left_part, right_part, preferred_element_type=...  11.4 us
    all_to_all x1, starting transfers between devices, per_device(): lax.all_to_all(outgoing_rows, FSDP, split_axis=0, concat_axis=0, tiled=True)  8.34 us
    gather x1, local copies, waits for them, and re-layouts, per_device(): right_part = jnp.take(cot_bands, owner_table % col_bands, axis=1)  7.74 us
    reshape x1, local copies, waits for them, and re-layouts, per_device(): cot_bands = full_cot.reshape(tokens_here, col_bands, block_size)  6.44 us
    ppermute x3, starting transfers between devices, per_device(): from_right = lax.ppermute(from_right, 'tensor', backward)  5.43 us
  transfers between devices with their start and end apart: 10, of which 7 were waited for; matrix products, arithmetic and copies ran while one was open for 8% of the time, Pallas kernels for 0%

profile of v1, /device:TPU:2, one launch (start us, length us, event | category | flops | bytes accessed | tf_op | source)
XLA Modules:
  0.0 241.7 jit_solution(16408934852915558418)
XLA Ops:
  7.2 0.0 reduce-scatter.3.cloned.1.call-start
  7.2 1.3 copy.42
  8.5 1.7 collective-permute-start.1
  10.3 6.9 %collective-permute-done = bf16[256,1024]{0,1:T(8,128)(2,1)S(1)} collective-permute-done((bf16[256,1024]{0,1:T(8,128)(2,1)S(1)}, bf16[256,1024]{0,1:T(8,128)(2,1)S(1)}, u32[]{:S(2)}, u32[]{:S(2)}) %collective-permute-start) | collective-permute-done | bytes 524320 | tf_op jit(solution)/shard_map/ppermute | solution.py:31
  17.2 2.0 collective-permute-start.3
  19.2 0.7 fusion.29
  19.8 5.9 %collective-permute-done.2 = bf16[256,1024]{0,1:T(8,128)(2,1)S(1)} collective-permute-done((bf16[256,1024]{0,1:T(8,128)(2,1)S(1)}, bf16[256,1024]{0,1:T(8,128)(2,1)S(1)}, u32[]{:S(2)}, u32[]{:S(2)}) %collective-permute-start.2) | collective-permute-done | bytes 524320 | tf_op jit(solution)/shard_map/ppermute | solution.py:31
  25.9 1.1 copy.40
  27.0 0.1 copy.41
  27.2 5.4 %gather_fusion = bf16[64,256,256]{2,1,0:T(8,128)(2,1)} fusion(bf16[256,2,256]{2,0,1:T(8,128)(2,1)S(1)} %copy.41, s32[1024]{0:T(1024)S(1)} %get-tuple-element.13), kind=kCustom, calls=%fused_computation | custom fusion | bytes 16777472 | tf_op jit(solution)/shard_map/jit(_take)/gather | solution.py:53
  32.5 2.2 broadcast_in_dim.69
  34.8 0.8 constant_dynamic-update-slice_fusion.7
  35.6 1.7 collective-permute-start.5
  37.3 0.9 constant_dynamic-update-slice_fusion.6
  38.2 0.8 constant_dynamic-update-slice_fusion.5
  39.0 0.9 constant_dynamic-update-slice_fusion.4
  39.9 0.8 constant_dynamic-update-slice_fusion.3
  40.7 1.9 constant_dynamic-update-slice_fusion.2
  42.6 1.4 collective-permute-done.5
  44.0 0.8 constant_dynamic-update-slice_fusion.1
  44.8 3.6 %collective-permute-done.6 = bf16[256,1024]{0,1:T(8,128)(2,1)S(1)} collective-permute-done((bf16[256,1024]{0,1:T(8,128)(2,1)}, bf16[256,1024]{0,1:T(8,128)(2,1)S(1)}, u32[]{:S(2)}, u32[]{:S(2)}) %collective-permute-start.6) | collective-permute-done | bytes 524320 | tf_op jit(solution)/shard_map/ppermute | solution.py:31
  48.4 0.8 constant_dynamic-update-slice_fusion
  49.2 6.4 %copy.45 = bf16[256,32,256]{2,0,1:T(8,128)(2,1)} copy(bf16[256,32,256]{0,2,1:T(8,128)(2,1)} %bitcast.6) | data formatting | bytes 8388608 | tf_op jit(solution)/shard_map/reshape | solution.py:52
  55.7 7.7 %gather_fusion.1 = bf16[64,256,256]{2,1,0:T(8,128)(2,1)} fusion(bf16[256,32,256]{2,0,1:T(8,128)(2,1)} %copy.45, s32[1024]{0:T(1024)S(1)} %get-tuple-element.12), kind=kCustom, calls=%fused_computation.1 | custom fusion | bytes 16777472 | tf_op jit(solution)/shard_map/jit(_take)/gather | solution.py:54
  63.4 11.4 %fusion.7 = bf16[64,256,256]{2,1,0:T(8,128)(2,1)} fusion(bf16[64,256,256]{2,1,0:T(8,128)(2,1)} %gather_fusion.1, pred[64]{0:T(512)(128)(4,1)S(1)} %get-tuple-element.7, bf16[64,256,256]{2,1,0:T(8,128)(2,1)} %gather_fusion, pred[64]{0:T(512)(128)(4,1)S(1)} %get-tuple-element.6), kind=kOutput, calls=%fused_computation.11 | convolution fusion | flops 2160066560 | bytes 25165952 | tf_op jit(solution)/shard_map/tnb,tnc->nbc/dot_general | solution.py:55
  74.8 0.0 reduce-scatter.5.cloned.1.call-start
  74.8 98.9 %reduce-scatter.3.cloned.1.call-done = bf16[2048,256]{1,0:T(8,128)(2,1)} async-done(((bf16[16384,256]{1,0:T(8,128)(2,1)}), bf16[2048,256]{1,0:T(8,128)(2,1)}) %reduce-scatter.3.cloned.1.call-update) | async-done | bytes 1048592 | tf_op jit(solution)/shard_map/reduce_scatter | solution.py:14
  173.8 0.1 and_select_fusion.1
  173.8 0.1 compare_convert_fusion
  173.9 0.1 copy.50
  174.0 27.2 %reduce-scatter.5.cloned.1.call-done = bf16[512,256]{1,0:T(8,128)(2,1)} async-done(((bf16[2048,256]{1,0:T(8,128)(2,1)}), bf16[512,256]{1,0:T(8,128)(2,1)}) %reduce-scatter.5.cloned.1.call-update) | async-done | bytes 262160 | tf_op jit(solution)/shard_map/reduce_scatter | solution.py:14
  201.3 1.8 broadcast_multiply_fusion
  203.1 1.4 fusion.27
  204.5 0.1 reduce_sum.39
  204.7 1.4 fusion.25
  206.1 0.8 multiply_reduce_fusion
  206.9 0.1 multiply_convert_fusion
  207.0 0.6 gather_fusion.2
  207.6 1.0 select_multiply_fusion
  208.5 8.3 %all-to-all-start = ((bf16[32,2,16,256]{3,2,1,0:T(8,128)(2,1)}), bf16[32,2,16,256]{3,2,1,0:T(8,128)(2,1)S(1)}, u32[]{:S(2)}, u32[]{:S(2)}) async-start(bf16[32,2,16,256]{3,2,1,0:T(8,128)(2,1)} %select_multiply_fusion), calls=%async_computation.2 | async-start | bytes 1048576 | tf_op jit(solution)/shard_map/all_to_all | solution.py:80
  216.9 0.2 select_reduce_fusion
  217.1 1.1 fusion.14
  218.2 1.1 fusion.16
  219.3 14.0 %all-to-all-done = bf16[32,2,16,256]{3,2,1,0:T(8,128)(2,1)S(1)} async-done(((bf16[32,2,16,256]{3,2,1,0:T(8,128)(2,1)}), bf16[32,2,16,256]{3,2,1,0:T(8,128)(2,1)S(1)}, u32[]{:S(2)}, u32[]{:S(2)}) %all-to-all-start) | async-done | bytes 524320 | tf_op jit(solution)/shard_map/all_to_all | solution.py:80
  233.3 0.6 gather_fusion.3
  233.9 0.1 select_bitcast_fusion
  234.0 0.1 copy.51
  234.1 0.8 broadcast_in_dim_reshape.3
  (39 shorter events, 0.2 us)
Async XLA Ops:
  7.2 198.9 %copy-start = (f32[1,2,256,256]{3,2,1,0:T(8,128)S(1)}, f32[1,2,256,256]{3,2,1,0:T(8,128)}, u32[]{:S(2)}) copy-start(f32[1,2,256,256]{3,2,1,0:T(8,128)} %param.14) | copy-start | bytes 1572868
  7.2 166.5 %reduce-scatter.3.cloned.1.call-start = ((), (), s32[]{:S(2)}) async-start(), calls=%async_computation.3 | async-start | bytes 9437184 | tf_op jit(solution)/shard_map/reduce_scatter | solution.py:14
  8.5 8.6 %collective-permute-start = (bf16[256,1024]{0,1:T(8,128)(2,1)S(1)}, bf16[256,1024]{0,1:T(8,128)(2,1)S(1)}, u32[]{:S(2)}, u32[]{:S(2)}) collective-permute-start(bf16[256,1024]{0,1:T(8,128)(2,1)S(1)} %copy.42), channel_id=1, source_target_pairs={{0,1},{1,2},{2,3},{3,4},{4,5},{5,6},{6,7},{7,0},{8,9},{9,10},{10,1... | collective-permute-start | bytes 1572872 | tf_op jit(solution)/shard_map/ppermute | solution.py:31
  8.5 8.6 %collective-permute-start.1 = (bf16[256,1024]{0,1:T(8,128)(2,1)S(1)}, bf16[256,1024]{0,1:T(8,128)(2,1)S(1)}, u32[]{:S(2)}, u32[]{:S(2)}) collective-permute-start(bf16[256,1024]{0,1:T(8,128)(2,1)S(1)} %copy.42), channel_id=1, source_target_pairs={{0,7},{1,0},{2,1},{3,2},{4,3},{5,4},{6,5},{7,6},{8,15},{9,8},{10,9... | collective-permute-start | bytes 1572872 | tf_op jit(solution)/shard_map/ppermute | solution.py:36
  17.1 8.6 %copy-start.6 = (bf16[256,1024]{0,1:T(8,128)(2,1)}, bf16[256,1024]{0,1:T(8,128)(2,1)S(1)}, u32[]{:S(2)}) copy-start(bf16[256,1024]{0,1:T(8,128)(2,1)S(1)} %collective-permute-done) | copy-start | bytes 1572868
  17.1 8.6 %collective-permute-start.2 = (bf16[256,1024]{0,1:T(8,128)(2,1)S(1)}, bf16[256,1024]{0,1:T(8,128)(2,1)S(1)}, u32[]{:S(2)}, u32[]{:S(2)}) collective-permute-start(bf16[256,1024]{0,1:T(8,128)(2,1)S(1)} %collective-permute-done), channel_id=1, source_target_pairs={{0,1},{1,2},{2,3},{3,4},{4,5},{5,6},{6,7},{7,0},{8,9},{9,10},{10,1... | collective-permute-start | bytes 1572872 | tf_op jit(solution)/shard_map/ppermute | solution.py:31
  17.2 18.5 %collective-permute-start.3 = (bf16[256,1024]{0,1:T(8,128)(2,1)S(1)}, bf16[256,1024]{0,1:T(8,128)(2,1)S(1)}, u32[]{:S(2)}, u32[]{:S(2)}) collective-permute-start(bf16[256,1024]{0,1:T(8,128)(2,1)S(1)} %collective-permute-done.1), channel_id=1, source_target_pairs={{0,7},{1,0},{2,1},{3,2},{4,3},{5,4},{6,5},{7,6},{8,15},{9,8},{10,9... | collective-permute-start | bytes 1572872 | tf_op jit(solution)/shard_map/ppermute | solution.py:36
  25.8 12.4 %collective-permute-start.4 = (bf16[256,1024]{0,1:T(8,128)(2,1)S(1)}, bf16[256,1024]{0,1:T(8,128)(2,1)}, u32[]{:S(2)}, u32[]{:S(2)}) collective-permute-start(bf16[256,1024]{0,1:T(8,128)(2,1)S(1)} %collective-permute-done.2), channel_id=1, source_target_pairs={{0,1},{1,2},{2,3},{3,4},{4,5},{5,6},{6,7},{7,0},{8,9},{9,10},{10,1... | collective-permute-start | bytes 1572872 | tf_op jit(solution)/shard_map/ppermute | solution.py:31
  32.5 3.1 %copy-start.8 = (s32[1,64]{1,0:T(1,128)S(1)}, s32[1,64]{1,0:T(1,128)}, u32[]{:S(2)}) copy-start(s32[1,64]{1,0:T(1,128)} %param.10) | copy-start | bytes 772
  32.5 4.8 %copy-start.7 = (bf16[256,1024]{0,1:T(8,128)(2,1)S(1)}, bf16[256,1024]{0,1:T(8,128)(2,1)}, u32[]{:S(2)}) copy-start(bf16[256,1024]{0,1:T(8,128)(2,1)} %copy-done.6) | copy-start | bytes 1572868
  35.6 8.4 %collective-permute-start.5 = (bf16[256,1024]{0,1:T(8,128)(2,1)S(1)}, bf16[256,1024]{0,1:T(8,128)(2,1)S(1)}, u32[]{:S(2)}, u32[]{:S(2)}) collective-permute-start(bf16[256,1024]{0,1:T(8,128)(2,1)S(1)} %collective-permute-done.3), channel_id=1, source_target_pairs={{0,7},{1,0},{2,1},{3,2},{4,3},{5,4},{6,5},{7,6},{8,15},{9,8},{10,9... | collective-permute-start | bytes 1572872 | tf_op jit(solution)/shard_map/ppermute | solution.py:36
  38.2 10.2 %collective-permute-start.6 = (bf16[256,1024]{0,1:T(8,128)(2,1)}, bf16[256,1024]{0,1:T(8,128)(2,1)S(1)}, u32[]{:S(2)}, u32[]{:S(2)}) collective-permute-start(bf16[256,1024]{0,1:T(8,128)(2,1)} %collective-permute-done.4), channel_id=1, source_target_pairs={{0,1},{1,2},{2,3},{3,4},{4,5},{5,6},{6,7},{7,0},{8,9},{9,10},{10,1... | collective-permute-start | bytes 1572872 | tf_op jit(solution)/shard_map/ppermute | solution.py:31
  74.8 126.5 %copy-start.2 = (f32[1,2,256,256]{3,2,1,0:T(8,128)S(1)}, f32[1,2,256,256]{3,2,1,0:T(8,128)}, u32[]{:S(2)}) copy-start(f32[1,2,256,256]{3,2,1,0:T(8,128)} %param.15) | copy-start | bytes 1572868
  74.8 129.9 %copy-start.5 = (f32[1,2,256,256]{3,2,1,0:T(8,128)S(1)}, f32[1,2,256,256]{3,2,1,0:T(8,128)}, u32[]{:S(2)}) copy-start(f32[1,2,256,256]{3,2,1,0:T(8,128)} %param.13) | copy-start | bytes 1572868
  74.8 126.5 %reduce-scatter.5.cloned.1.call-start = ((), (), s32[]{:S(2)}) async-start(), calls=%async_computation.4 | async-start | bytes 1310720 | tf_op jit(solution)/shard_map/reduce_scatter | solution.py:14
  203.1 14.0 %copy-start.1 = (bf16[512,256]{1,0:T(8,128)(2,1)S(1)}, bf16[512,256]{1,0:T(8,128)(2,1)}, u32[]{:S(2)}) copy-start(bf16[512,256]{1,0:T(8,128)(2,1)} %reduce-scatter.5.cloned.1.call-done) | copy-start | bytes 786436
  203.1 14.0 %copy-start.3 = (f32[1,2,256,256]{3,2,1,0:T(8,128)S(1)}, f32[1,2,256,256]{3,2,1,0:T(8,128)}, u32[]{:S(2)}) copy-start(f32[1,2,256,256]{3,2,1,0:T(8,128)} %param.12) | copy-start | bytes 1572868
  204.7 13.5 %copy-start.4 = (f32[1,2,256,256]{3,2,1,0:T(8,128)S(1)}, f32[1,2,256,256]{3,2,1,0:T(8,128)}, u32[]{:S(2)}) copy-start(f32[1,2,256,256]{3,2,1,0:T(8,128)} %param.11) | copy-start | bytes 1572868
  208.5 24.8 %all-to-all-start = ((bf16[32,2,16,256]{3,2,1,0:T(8,128)(2,1)}), bf16[32,2,16,256]{3,2,1,0:T(8,128)(2,1)S(1)}, u32[]{:S(2)}, u32[]{:S(2)}) async-start(bf16[32,2,16,256]{3,2,1,0:T(8,128)(2,1)} %select_multiply_fusion), calls=%async_computation.2 | async-start | bytes 1048576 | tf_op jit(solution)/shard_map/all_to_all | solution.py:80
Sparse Core Ops, SparseCore 0:
  74.9 98.7 reduce-scatter.2
  176.3 24.9 reduce-scatter.4
